TPU v7x, 32 devices: a whole 2x2x4 slice. The times are simulated.
32 devices in a mesh: seq: 8 (over z, x), tp: 4 (over y, core).
Axes of the slice: x: 2, y: 2, z: 4, core: 2. Of those that a mesh axis runs over, the one named last changes fastest.
Arguments:
- hidden_in: bfloat16 [16, 2048], replicated, may hold values from -6 to 6
- lengths: int32 [16], replicated, may hold values from 1 to 511, 2431 in all
- positions: int32 [16], replicated, may hold values from 0 to 1023
- query_weight: bfloat16 [2, 2048, 2048], P(None, 'seq', 'tp'), may hold values from -0.125 to 0.125
- key_weight: bfloat16 [2, 2048, 512], P(None, 'seq', 'tp'), may hold values from -4 to 4
- value_weight: bfloat16 [2, 2048, 512], P(None, 'seq', 'tp'), may hold values from -0.125 to 0.125
- out_weight: bfloat16 [2, 2048, 2048], P(None, 'tp', 'seq'), may hold values from -0.125 to 0.125
- gate_weight: bfloat16 [2, 2048, 8192], P(None, 'seq', 'tp'), may hold values from -0.125 to 0.125
- up_weight: bfloat16 [2, 2048, 8192], P(None, 'seq', 'tp'), may hold values from -0.125 to 0.125
- down_weight: bfloat16 [2, 8192, 2048], P(None, 'tp', 'seq'), may hold values from -0.0625 to 0.0625
- key_cache: bfloat16 [2, 16, 512, 512], P(None, None, 'seq', 'tp'), may hold values from -80 to 80
- value_cache: bfloat16 [2, 16, 512, 512], P(None, None, 'seq', 'tp'), may hold values from -6 to 6
Outputs:
- hidden_out: bfloat16 [16, 2048], replicated
- key_out: bfloat16 [2, 16, 512, 512], P(None, None, 'seq', 'tp')
- value_out: bfloat16 [2, 16, 512, 512], P(None, None, 'seq', 'tp')
Inputs may be any that keep to these rules, and one draw needn't show every extreme that they name: Request b has its cached rows at positions 0 .. lengths[b] - 1 and its new token goes to row lengths[b]; rows above are padding. The longest request has exactly 511 cached rows.
All inputs are finite; a program needn't handle non-finite values.
Results may differ from a plain program's by a relative error of at most 0.015.
Values may be sent and summed in bfloat16 or wider, within the bound.
No kernel may reach another device: no remote copies, remote signals or barrier semaphores. Data moves between devices by JAX's collectives and lax.ppermute only.
A program may use at most 64 MiB of HBM per device.

v0:
```python
import math
import jax
import jax.numpy as jnp
from jax import lax
from jax.sharding import PartitionSpec as P

HEAD_DIM = 64
LAYERS = 2
eps_norm = 1e-05
neg_fill = -1e30


def rms_norm(stream):
    as_float = stream.astype(jnp.float32)
    spread = jnp.mean(as_float * as_float, axis=-1, keepdims=True)
    return (as_float * lax.rsqrt(spread + eps_norm)).astype(jnp.bfloat16)


def rotate(heads, positions):
    half_dim = heads.shape[-1] // 2
    inverse = 500000.0 ** (-(2.0 * jnp.arange(half_dim, dtype=jnp.float32)) / heads.shape[-1])
    angles = positions.astype(jnp.float32)[:, None] * inverse[None, :]
    cosine = jnp.cos(angles)[:, None, :]
    sine = jnp.sin(angles)[:, None, :]
    first_half = heads[..., :half_dim]
    second_half = heads[..., half_dim:]
    return jnp.concatenate(
        [first_half * cosine - second_half * sine, second_half * cosine + first_half * sine],
        axis=-1,
    )


def per_device(
    hidden_in,
    lengths,
    positions,
    query_weight,
    key_weight,
    value_weight,
    out_weight,
    gate_weight,
    up_weight,
    down_weight,
    key_cache,
    value_cache,
):
    seq_index = lax.axis_index("seq")
    row_count = query_weight.shape[1]
    row_start = seq_index * row_count
    col_count = out_weight.shape[2]
    col_start = seq_index * col_count
    block_len = key_cache.shape[2]
    kv_width_here = key_cache.shape[3]
    query_width = query_weight.shape[2]
    requests = hidden_in.shape[0]
    group_heads = query_width // HEAD_DIM
    kv_here = kv_width_here // HEAD_DIM
    repeat = group_heads // kv_here
    score_scale = 1.0 / math.sqrt(HEAD_DIM)
    global_slots = seq_index * block_len + jnp.arange(block_len, dtype=jnp.int32)
    new_slot = (global_slots[None, :] == lengths[:, None])[:, :, None]
    live_mask = (global_slots[None, :] <= lengths[:, None])[:, None, None, :]

    def finish(part_terms, stream_now):
        summed = lax.psum(part_terms, "tp")
        own_cols = lax.dynamic_slice_in_dim(stream_now, col_start, col_count, 1).astype(jnp.float32)
        return lax.all_gather((own_cols + summed).astype(jnp.bfloat16), "seq", axis=1, tiled=True)

    stream = hidden_in
    key_layers = []
    value_layers = []
    for layer_idx in range(LAYERS):
        normed = rms_norm(stream)
        own_rows = lax.dynamic_slice_in_dim(normed, row_start, row_count, 1)
        query_part = jnp.dot(own_rows, query_weight[layer_idx], preferred_element_type=jnp.float32)
        key_part = jnp.dot(own_rows, key_weight[layer_idx], preferred_element_type=jnp.float32)
        value_part = jnp.dot(own_rows, value_weight[layer_idx], preferred_element_type=jnp.float32)
        query, key_new, value_new = lax.psum((query_part, key_part, value_part), "seq")
        query = rotate(query.reshape(requests, group_heads, HEAD_DIM), positions).astype(
            jnp.bfloat16
        )
        query = query.reshape(requests, kv_here, repeat, HEAD_DIM)
        key_new = (
            rotate(key_new.reshape(requests, kv_here, HEAD_DIM), positions)
            .astype(jnp.bfloat16)
            .reshape(requests, kv_width_here)
        )
        value_new = value_new.astype(jnp.bfloat16)
        key_rows = jnp.where(new_slot, key_new[:, None, :], key_cache[layer_idx])
        value_rows = jnp.where(new_slot, value_new[:, None, :], value_cache[layer_idx])
        key_heads = key_rows.reshape(requests, block_len, kv_here, HEAD_DIM)
        value_heads = value_rows.reshape(requests, block_len, kv_here, HEAD_DIM)
        scores = (
            jnp.einsum("bkrd,bskd->bkrs", query, key_heads, preferred_element_type=jnp.float32)
            * score_scale
        )
        scores = jnp.where(live_mask, scores, neg_fill)
        row_top = lax.pmax(jnp.max(scores, axis=3), "seq")
        weights = jnp.where(live_mask, jnp.exp(scores - row_top[..., None]), 0.0)
        local_sums = jnp.sum(weights, axis=3)
        local_acc = jnp.einsum(
            "bkrs,bskd->bkrd",
            weights.astype(jnp.bfloat16),
            value_heads,
            preferred_element_type=jnp.float32,
        )
        totals, weighted = lax.psum((local_sums, local_acc), "seq")
        attended = (
            (weighted / totals[..., None]).astype(jnp.bfloat16).reshape(requests, query_width)
        )
        attn_terms = jnp.dot(attended, out_weight[layer_idx], preferred_element_type=jnp.float32)
        mid = finish(attn_terms, stream)
        normed_two = rms_norm(mid)
        rows_two = lax.dynamic_slice_in_dim(normed_two, row_start, row_count, 1)
        gate_part = jnp.dot(rows_two, gate_weight[layer_idx], preferred_element_type=jnp.float32)
        up_part = jnp.dot(rows_two, up_weight[layer_idx], preferred_element_type=jnp.float32)
        gate_sum, up_sum = lax.psum((gate_part, up_part), "seq")
        hidden = (jax.nn.silu(gate_sum) * up_sum).astype(jnp.bfloat16)
        down_terms = jnp.dot(hidden, down_weight[layer_idx], preferred_element_type=jnp.float32)
        stream = finish(down_terms, mid)
        key_layers.append(key_rows)
        value_layers.append(value_rows)
    return (stream, jnp.stack(key_layers), jnp.stack(value_layers))


def solution(mesh):
    return jax.shard_map(
        per_device,
        mesh=mesh,
        in_specs=(
            P(),
            P(),
            P(),
            P(None, "seq", "tp"),
            P(None, "seq", "tp"),
            P(None, "seq", "tp"),
            P(None, "tp", "seq"),
            P(None, "seq", "tp"),
            P(None, "seq", "tp"),
            P(None, "tp", "seq"),
            P(None, None, "seq", "tp"),
            P(None, None, "seq", "tp"),
        ),
        out_specs=(P(), P(None, None, "seq", "tp"), P(None, None, "seq", "tp")),
        check_vma=False,
    )
```

profile of v0, /device:TPU:0, one launch (start us, length us, event | category | flops | bytes accessed | tf_op | source)
XLA Modules:
  0.0 562.6 jit_solution(6855281874656980006)
XLA Ops:
  7.2 0.9 convert_element_type.105
  8.1 1.0 multiply_reduce_fusion.3
  9.1 1.0 fusion.46
  10.2 1.0 fusion.48
  11.3 1.1 fusion.32
  12.5 1.0 slice.86
  13.7 39.8 %all-reduce.3 = (bf16[16,128]{1,0:T(8,128)(2,1)S(1)}, f32[16,2,64]{2,1,0:T(2,128)S(1)}, f32[16,8,64]{2,1,0:T(8,128)S(1)}) all-reduce(f32[16,128]{1,0:T(8,128)S(1)} %fusion.46, f32[16,2,64]{2,1,0:T(2,128)S(1)} %reshape.206, f32[16,8,64]{2,1,0:T(8,128)S(1)} %reshape.205), channel_id=1, replica_groups=mesh['seq'=8,'tp'=4] {'seq'}, use_global_device_ids=true, to_apply=%region_5.6 | all-reduce | flops 12288 | bytes 94208 | tf_op jit(solution)/shard_map/psum | solution.py:78
  53.6 0.7 broadcast_in_dim.117
  54.3 1.1 squeeze.56
  55.8 1.7 fusion.88
  57.5 33.0 %pmax.14 = f32[16,2,4]{2,1,0:T(2,128)S(1)} all-reduce(f32[16,2,4]{2,1,0:T(2,128)S(1)} %get-tuple-element.38), channel_id=1, replica_groups=mesh['seq'=8,'tp'=4] {'seq'}, use_global_device_ids=true, to_apply=%region_4.5 | all-reduce | flops 128 | bytes 1024 | tf_op jit(solution)/shard_map/pmax | solution.py:98
  90.7 1.0 fusion.21
  91.8 33.8 %all-reduce.2 = (f32[16,2,4,64]{3,2,1,0:T(4,128)S(1)}, f32[16,2,4]{2,1,0:T(2,128)S(1)}) all-reduce(f32[16,2,4,64]{3,2,1,0:T(4,128)S(1)} %fusion.21, f32[16,2,4]{2,1,0:T(2,128)S(1)} %fusion.56), channel_id=1, replica_groups=mesh['seq'=8,'tp'=4] {'seq'}, use_global_device_ids=true, to_apply=%region_6.7 | all-reduce | flops 8320 | bytes 66560 | tf_op jit(solution)/shard_map/psum | solution.py:107
  126.0 10.1 %psum.131 = f32[16,256]{1,0:T(8,128)S(1)} all-reduce(f32[16,256]{1,0:T(8,128)S(1)} %fusion.30), channel_id=1, replica_groups=mesh['seq'=8,'tp'=4] {'tp'}, use_global_device_ids=true, to_apply=%region_9.10 | all-reduce | flops 4096 | bytes 32768 | tf_op jit(solution)/shard_map/psum | solution.py:65
  136.1 0.7 add_convert_fusion.5
  136.8 30.5 %all_gather.12 = bf16[16,2048]{1,0:T(8,128)(2,1)S(1)} all-gather(bf16[16,256]{1,0:T(8,128)(2,1)S(1)} %add_convert_fusion.5), channel_id=1, replica_groups=mesh['seq'=8,'tp'=4] {'seq'}, dimensions={1}, use_global_device_ids=true | all-gather | bytes 73728 | tf_op jit(solution)/shard_map/all_gather | solution.py:67
  167.5 1.0 fusion.10
  168.4 2.3 fusion.12
  170.8 0.7 convert_element_type.131
  171.4 69.2 %all-reduce.11.cloned.1.call-done = (f32[16,2048]{1,0:T(8,128)}, f32[16,2048]{1,0:T(8,128)}) async-done(((f32[16,2048]{1,0:T(8,128)}, f32[16,2048]{1,0:T(8,128)}), (f32[16,2048]{1,0:T(8,128)}, f32[16,2048]{1,0:T(8,128)})) %all-reduce.11.cloned.1.call-update) | async-done | bytes 262160 | tf_op jit(solution)/shard_map/psum | solution.py:117
  240.6 1.6 fusion.8
  242.2 10.1 %psum.134 = f32[16,256]{1,0:T(8,128)S(1)} all-reduce(f32[16,256]{1,0:T(8,128)S(1)} %fusion.8), channel_id=1, replica_groups=mesh['seq'=8,'tp'=4] {'tp'}, use_global_device_ids=true, to_apply=%region_13.14 | all-reduce | flops 4096 | bytes 32768 | tf_op jit(solution)/shard_map/psum | solution.py:65
  252.3 30.5 %all_gather.13 = bf16[16,2048]{1,0:T(8,128)(2,1)S(1)} all-gather(bf16[16,256]{1,0:T(8,128)(2,1)S(1)} %add_convert_fusion.4), channel_id=1, replica_groups=mesh['seq'=8,'tp'=4] {'seq'}, dimensions={1}, use_global_device_ids=true | all-gather | bytes 73728 | tf_op jit(solution)/shard_map/all_gather | solution.py:67
  283.0 1.0 fusion.42
  284.0 1.0 fusion.44
  285.1 1.1 fusion.28
  286.4 36.4 %all-reduce.1 = (bf16[16,128]{1,0:T(8,128)(2,1)S(1)}, f32[16,2,64]{2,1,0:T(2,128)S(1)}, f32[16,8,64]{2,1,0:T(8,128)S(1)}) all-reduce(f32[16,128]{1,0:T(8,128)S(1)} %fusion.42, f32[16,2,64]{2,1,0:T(2,128)S(1)} %reshape.209, f32[16,8,64]{2,1,0:T(8,128)S(1)} %reshape.208), channel_id=1, replica_groups=mesh['seq'=8,'tp'=4] {'seq'}, use_global_device_ids=true, to_apply=%region_19.20 | all-reduce | flops 12288 | bytes 94208 | tf_op jit(solution)/shard_map/psum | solution.py:78
  323.0 0.7 convert_element_type.132
  323.7 0.7 broadcast_in_dim.120
  324.4 1.9 broadcast_select_fusion.1
  326.2 1.2 squeeze.67
  327.4 0.2 squeeze.65
  327.8 1.2 fusion.89
  329.0 33.0 %pmax.15 = f32[16,2,4]{2,1,0:T(2,128)S(1)} all-reduce(f32[16,2,4]{2,1,0:T(2,128)S(1)} %get-tuple-element.40), channel_id=1, replica_groups=mesh['seq'=8,'tp'=4] {'seq'}, use_global_device_ids=true, to_apply=%region_18.19 | all-reduce | flops 128 | bytes 1024 | tf_op jit(solution)/shard_map/pmax | solution.py:98
  362.0 0.9 fusion.58
  362.9 1.1 fusion.20
  364.0 34.0 %all-reduce = (f32[16,2,4,64]{3,2,1,0:T(4,128)S(1)}, f32[16,2,4]{2,1,0:T(2,128)S(1)}) all-reduce(f32[16,2,4,64]{3,2,1,0:T(4,128)S(1)} %fusion.20, f32[16,2,4]{2,1,0:T(2,128)S(1)} %fusion.58), channel_id=1, replica_groups=mesh['seq'=8,'tp'=4] {'seq'}, use_global_device_ids=true, to_apply=%region_20.21 | all-reduce | flops 8320 | bytes 66560 | tf_op jit(solution)/shard_map/psum | solution.py:107
  398.2 1.1 fusion.26
  399.3 10.1 %psum.140 = f32[16,256]{1,0:T(8,128)S(1)} all-reduce(f32[16,256]{1,0:T(8,128)S(1)} %fusion.26), channel_id=1, replica_groups=mesh['seq'=8,'tp'=4] {'tp'}, use_global_device_ids=true, to_apply=%region_23.24 | all-reduce | flops 4096 | bytes 32768 | tf_op jit(solution)/shard_map/psum | solution.py:65
  409.4 30.5 %all_gather.14 = bf16[16,2048]{1,0:T(8,128)(2,1)S(1)} all-gather(bf16[16,256]{1,0:T(8,128)(2,1)S(1)} %add_convert_fusion.3), channel_id=1, replica_groups=mesh['seq'=8,'tp'=4] {'seq'}, dimensions={1}, use_global_device_ids=true | all-gather | bytes 73728 | tf_op jit(solution)/shard_map/all_gather | solution.py:67
  440.0 0.9 fusion.4
  441.0 2.3 fusion.6
  443.4 1.1 pad_maximum_fusion
  444.4 68.8 %all-reduce.9.cloned.1.call-done = (f32[16,2048]{1,0:T(8,128)}, f32[16,2048]{1,0:T(8,128)}) async-done(((f32[16,2048]{1,0:T(8,128)}, f32[16,2048]{1,0:T(8,128)}), (f32[16,2048]{1,0:T(8,128)}, f32[16,2048]{1,0:T(8,128)})) %all-reduce.9.cloned.1.call-update) | async-done | bytes 262160 | tf_op jit(solution)/shard_map/psum | solution.py:117
  513.3 1.2 fusion.2
  514.5 10.1 %psum.143 = f32[16,256]{1,0:T(8,128)S(1)} all-reduce(f32[16,256]{1,0:T(8,128)S(1)} %fusion.2), channel_id=1, replica_groups=mesh['seq'=8,'tp'=4] {'tp'}, use_global_device_ids=true, to_apply=%region_27.28 | all-reduce | flops 4096 | bytes 32768 | tf_op jit(solution)/shard_map/psum | solution.py:65
  524.6 30.5 %all_gather.15 = bf16[16,2048]{1,0:T(8,128)(2,1)S(1)} all-gather(bf16[16,256]{1,0:T(8,128)(2,1)S(1)} %add_convert_fusion.2), channel_id=1, replica_groups=mesh['seq'=8,'tp'=4] {'seq'}, dimensions={1}, use_global_device_ids=true | all-gather | bytes 73728 | tf_op jit(solution)/shard_map/all_gather | solution.py:67
  555.1 0.6 copy.36
  (73 shorter events, 2.7 us)
Async XLA Ops:
  7.2 47.1 %slice-start = ((bf16[2,16,64,128]{3,2,1,0:T(8,128)(2,1)}), bf16[1,16,64,128]{3,2,1,0:T(8,128)(2,1)S(1)}, s32[]{:S(2)}) async-start(bf16[2,16,64,128]{3,2,1,0:T(8,128)(2,1)} %param.22), calls=%async_computation.2 | async-start | bytes 524288 | tf_op jit(solution)/shard_map/slice | solution.py:89
  7.2 48.1 %copy-start.15 = (s32[16]{0:T(128)S(1)}, s32[16]{0:T(128)}, u32[]{:S(2)}) copy-start(s32[16]{0:T(128)} %param.14) | copy-start | bytes 196
  7.2 48.5 %copy-start.13 = (s32[16]{0:T(128)S(1)}, s32[16]{0:T(128)}, u32[]{:S(2)}) copy-start(s32[16]{0:T(128)} %param.13) | copy-start | bytes 196
  7.2 233.4 %all-reduce.11.cloned.1.call-start = ((), (), s32[]{:S(2)}) async-start(), calls=%async_computation.1 | async-start | bytes 524288 | tf_op jit(solution)/shard_map/psum | solution.py:117
  53.6 0.7 copy-start.10
  54.3 71.6 %copy-start.7 = (bf16[2,512,256]{2,1,0:T(8,128)(2,1)S(1)}, bf16[2,512,256]{2,1,0:T(8,128)(2,1)}, u32[]{:S(2)}) copy-start(bf16[2,512,256]{2,1,0:T(8,128)(2,1)} %param.18) | copy-start | bytes 1572868
  55.5 111.9 %copy-start = (bf16[2,256,2048]{2,1,0:T(8,128)(2,1)S(1)}, bf16[2,256,2048]{2,1,0:T(8,128)(2,1)}, u32[]{:S(2)}) copy-start(bf16[2,256,2048]{2,1,0:T(8,128)(2,1)} %param.20) | copy-start | bytes 6291460
  55.7 112.7 %copy-start.9 = (pred[16,64]{1,0:T(8,128)(4,1)}, pred[16,64]{1,0:T(8,128)(4,1)S(1)}, u32[]{:S(2)}) copy-start(pred[16,64]{1,0:T(8,128)(4,1)S(1)} %get-tuple-element.34) | copy-start | bytes 3076
  55.7 112.7 %copy-start.12 = (pred[16,64]{1,0:T(8,128)(4,1)}, pred[16,64]{1,0:T(8,128)(4,1)S(1)}, u32[]{:S(2)}) copy-start(pred[16,64]{1,0:T(8,128)(4,1)S(1)} %get-tuple-element.35) | copy-start | bytes 3076
  168.4 155.9 %copy-start.1 = (bf16[2,16,64,128]{3,2,1,0:T(8,128)(2,1)S(1)}, bf16[2,16,64,128]{3,2,1,0:T(8,128)(2,1)}, u32[]{:S(2)}) copy-start(bf16[2,16,64,128]{3,2,1,0:T(8,128)(2,1)} %param.23) | copy-start | bytes 1572868
  168.4 155.9 %copy-start.2 = (bf16[2,16,64,128]{3,2,1,0:T(8,128)(2,1)S(1)}, bf16[2,16,64,128]{3,2,1,0:T(8,128)(2,1)}, u32[]{:S(2)}) copy-start(bf16[2,16,64,128]{3,2,1,0:T(8,128)(2,1)} %param.22) | copy-start | bytes 1572868
  170.7 342.6 %all-reduce.9.cloned.1.call-start = ((), (), s32[]{:S(2)}) async-start(), calls=%async_computation | async-start | bytes 524288 | tf_op jit(solution)/shard_map/psum | solution.py:117
  322.8 0.9 copy-start.11
  323.0 0.7 copy-start.8
  364.0 79.4 %copy-start.3 = (bf16[1,16,64,128]{3,2,1,0:T(8,128)(2,1)S(1)}, bf16[1,16,64,128]{3,2,1,0:T(8,128)(2,1)}, u32[]{:S(2)}) copy-start(bf16[1,16,64,128]{3,2,1,0:T(8,128)(2,1)} %get-tuple-element.17) | copy-start | bytes 786436
  364.0 79.4 %copy-start.4 = (bf16[1,16,64,128]{3,2,1,0:T(8,128)(2,1)S(1)}, bf16[1,16,64,128]{3,2,1,0:T(8,128)(2,1)}, u32[]{:S(2)}) copy-start(bf16[1,16,64,128]{3,2,1,0:T(8,128)(2,1)} %get-tuple-element.18) | copy-start | bytes 786436
  364.0 79.4 %copy-start.5 = (bf16[1,16,64,128]{3,2,1,0:T(8,128)(2,1)S(1)}, bf16[1,16,64,128]{3,2,1,0:T(8,128)(2,1)}, u32[]{:S(2)}) copy-start(bf16[1,16,64,128]{3,2,1,0:T(8,128)(2,1)} %get-tuple-element.32) | copy-start | bytes 786436
  364.0 79.4 %copy-start.6 = (bf16[1,16,64,128]{3,2,1,0:T(8,128)(2,1)S(1)}, bf16[1,16,64,128]{3,2,1,0:T(8,128)(2,1)}, u32[]{:S(2)}) copy-start(bf16[1,16,64,128]{3,2,1,0:T(8,128)(2,1)} %get-tuple-element.33) | copy-start | bytes 786436
  441.0 72.3 %copy-start.14 = (bf16[2,2048,256]{2,1,0:T(8,128)(2,1)S(1)}, bf16[2,2048,256]{2,1,0:T(8,128)(2,1)}, u32[]{:S(2)}) copy-start(bf16[2,2048,256]{2,1,0:T(8,128)(2,1)} %param.21) | copy-start | bytes 6291460
Sparse Core Ops, SparseCore 0:
  170.8 69.7 all-reduce.10
  443.5 69.7 all-reduce.8
where the time goes:
time: 564 us; the launch traced here: 563 us
  blocking collectives  372 us (66%)
  waiting for transfers between devices  138 us (24%)
  matrix products  22 us (4%)
  between operations  14.4 us (3%)
  other arithmetic  8.02 us (1%)
  local copies, waits for them, and re-layouts  7.62 us (1%)
    psum x2, waiting for transfers between devices, per_device(): gate_sum, up_sum = lax.psum((gate_part, up_part), 'seq')  138 us
    all_gather x4, blocking collectives, finish(): lax.all_gather((own_cols + summed).astype(jnp.bfloat16), 'seq', axis=1, t...  122 us
    psum x2, blocking collectives, per_device(): lax.psum((query_part, key_part, value_part), 'seq')  76.3 us
    psum x2, blocking collectives, per_device(): totals, weighted = lax.psum((local_sums, local_acc), 'seq')  67.8 us
    pmax x2, blocking collectives, per_device(): row_top = lax.pmax(jnp.max(scores, axis=3), 'seq')  66 us
    psum x4, blocking collectives, finish(): summed = lax.psum(part_terms, 'tp')  40.5 us
  transfers between devices with their start and end apart: 2, of which 2 were waited for; matrix products, arithmetic and copies ran while one was open for 0% of the time, Pallas kernels for 0%

commit v1 on v0

--- a/solution.py
+++ b/solution.py
@@ -62,7 +62,7 @@
     live_mask = (global_slots[None, :] <= lengths[:, None])[:, None, None, :]
 
     def finish(part_terms, stream_now):
-        summed = lax.psum(part_terms, "tp")
+        summed = jnp.sum(lax.all_gather(part_terms, "tp"), axis=0)
         own_cols = lax.dynamic_slice_in_dim(stream_now, col_start, col_count, 1).astype(jnp.float32)
         return lax.all_gather((own_cols + summed).astype(jnp.bfloat16), "seq", axis=1, tiled=True)
 

time: 564 us -> 544 us (0.965)
  blocking collectives: 372 us -> 353 us
    psum x4 -> x0, blocking collectives: 40.5 us -> none  [finish(): summed = lax.psum(part_terms, 'tp')]
    all_gather x0 -> x4, blocking collectives: none -> 21 us  [finish(): summed = jnp.sum(lax.all_gather(part_terms, 'tp'), axis=0)]
where the time goes in v1:
time: 544 us; the launch traced here: 543 us
  blocking collectives  353 us (65%)
  waiting for transfers between devices  138 us (25%)
  matrix products  22 us (4%)
  between operations  14.4 us (3%)
  other arithmetic  8.05 us (1%)
  local copies, waits for them, and re-layouts  7.62 us (1%)
    psum x2, waiting for transfers between devices, per_device(): gate_sum, up_sum = lax.psum((gate_part, up_part), 'seq')  138 us
    all_gather x4, blocking collectives, finish(): lax.all_gather((own_cols + summed).astype(jnp.bfloat16), 'seq', axis=1, t...  122 us
    psum x2, blocking collectives, per_device(): lax.psum((query_part, key_part, value_part), 'seq')  76.3 us
    psum x2, blocking collectives, per_device(): totals, weighted = lax.psum((local_sums, local_acc), 'seq')  67.8 us
    pmax x2, blocking collectives, per_device(): row_top = lax.pmax(jnp.max(scores, axis=3), 'seq')  66 us
    all_gather x4, blocking collectives, finish(): summed = jnp.sum(lax.all_gather(part_terms, 'tp'), axis=0)  21 us
  transfers between devices with their start and end apart: 2, of which 2 were waited for; matrix products, arithmetic and copies ran while one was open for 0% of the time, Pallas kernels for 0%

profile of v1, /device:TPU:0, one launch (start us, length us, event | category | flops | bytes accessed | tf_op | source)
XLA Modules:
  0.0 542.9 jit_solution(15853808710176687632)
XLA Ops:
  7.2 0.9 convert_element_type.105
  8.1 1.0 multiply_reduce_fusion.3
  9.1 1.0 fusion.46
  10.2 1.0 fusion.48
  11.3 1.1 fusion.32
  12.5 1.0 slice.86
  13.7 39.8 %all-reduce.3 = (bf16[16,128]{1,0:T(8,128)(2,1)S(1)}, f32[16,2,64]{2,1,0:T(2,128)S(1)}, f32[16,8,64]{2,1,0:T(8,128)S(1)}) all-reduce(f32[16,128]{1,0:T(8,128)S(1)} %fusion.46, f32[16,2,64]{2,1,0:T(2,128)S(1)} %reshape.206, f32[16,8,64]{2,1,0:T(8,128)S(1)} %reshape.205), channel_id=1, replica_groups=mesh['seq'=8,'tp'=4] {'seq'}, use_global_device_ids=true, to_apply=%region_5.6 | all-reduce | flops 12288 | bytes 94208 | tf_op jit(solution)/shard_map/psum | solution.py:78
  53.6 0.7 broadcast_in_dim.117
  54.3 1.1 squeeze.56
  55.8 1.7 fusion.88
  57.5 33.0 %pmax.14 = f32[16,2,4]{2,1,0:T(2,128)S(1)} all-reduce(f32[16,2,4]{2,1,0:T(2,128)S(1)} %get-tuple-element.38), channel_id=1, replica_groups=mesh['seq'=8,'tp'=4] {'seq'}, use_global_device_ids=true, to_apply=%region_4.5 | all-reduce | flops 128 | bytes 1024 | tf_op jit(solution)/shard_map/pmax | solution.py:98
  90.7 1.0 fusion.21
  91.8 33.8 %all-reduce.2 = (f32[16,2,4,64]{3,2,1,0:T(4,128)S(1)}, f32[16,2,4]{2,1,0:T(2,128)S(1)}) all-reduce(f32[16,2,4,64]{3,2,1,0:T(4,128)S(1)} %fusion.21, f32[16,2,4]{2,1,0:T(2,128)S(1)} %fusion.56), channel_id=1, replica_groups=mesh['seq'=8,'tp'=4] {'seq'}, use_global_device_ids=true, to_apply=%region_6.7 | all-reduce | flops 8320 | bytes 66560 | tf_op jit(solution)/shard_map/psum | solution.py:107
  126.0 5.2 all-gather
  131.2 0.7 add_convert_fusion.5
  131.9 30.5 %all_gather.38 = bf16[16,2048]{1,0:T(8,128)(2,1)S(1)} all-gather(bf16[16,256]{1,0:T(8,128)(2,1)S(1)} %add_convert_fusion.5), channel_id=1, replica_groups=mesh['seq'=8,'tp'=4] {'seq'}, dimensions={1}, use_global_device_ids=true | all-gather | bytes 73728 | tf_op jit(solution)/shard_map/all_gather | solution.py:67
  162.6 1.0 fusion.10
  163.6 2.3 fusion.12
  165.9 0.7 convert_element_type.131
  166.6 69.1 %all-reduce.11.cloned.1.call-done = (f32[16,2048]{1,0:T(8,128)}, f32[16,2048]{1,0:T(8,128)}) async-done(((f32[16,2048]{1,0:T(8,128)}, f32[16,2048]{1,0:T(8,128)}), (f32[16,2048]{1,0:T(8,128)}, f32[16,2048]{1,0:T(8,128)})) %all-reduce.11.cloned.1.call-update) | async-done | bytes 262160 | tf_op jit(solution)/shard_map/psum | solution.py:117
  235.7 1.6 fusion.8
  237.3 5.2 all-gather.1
  242.5 30.5 %all_gather.41 = bf16[16,2048]{1,0:T(8,128)(2,1)S(1)} all-gather(bf16[16,256]{1,0:T(8,128)(2,1)S(1)} %add_convert_fusion.4), channel_id=1, replica_groups=mesh['seq'=8,'tp'=4] {'seq'}, dimensions={1}, use_global_device_ids=true | all-gather | bytes 73728 | tf_op jit(solution)/shard_map/all_gather | solution.py:67
  273.2 1.0 fusion.42
  274.2 1.0 fusion.44
  275.2 1.1 fusion.28
  276.5 36.5 %all-reduce.1 = (bf16[16,128]{1,0:T(8,128)(2,1)S(1)}, f32[16,2,64]{2,1,0:T(2,128)S(1)}, f32[16,8,64]{2,1,0:T(8,128)S(1)}) all-reduce(f32[16,128]{1,0:T(8,128)S(1)} %fusion.42, f32[16,2,64]{2,1,0:T(2,128)S(1)} %reshape.209, f32[16,8,64]{2,1,0:T(8,128)S(1)} %reshape.208), channel_id=1, replica_groups=mesh['seq'=8,'tp'=4] {'seq'}, use_global_device_ids=true, to_apply=%region_19.20 | all-reduce | flops 12288 | bytes 94208 | tf_op jit(solution)/shard_map/psum | solution.py:78
  313.2 0.7 convert_element_type.132
  313.9 0.7 broadcast_in_dim.120
  314.6 1.9 broadcast_select_fusion.1
  316.5 1.2 squeeze.67
  317.7 0.2 squeeze.65
  318.0 1.2 fusion.89
  319.3 33.0 %pmax.15 = f32[16,2,4]{2,1,0:T(2,128)S(1)} all-reduce(f32[16,2,4]{2,1,0:T(2,128)S(1)} %get-tuple-element.40), channel_id=1, replica_groups=mesh['seq'=8,'tp'=4] {'seq'}, use_global_device_ids=true, to_apply=%region_18.19 | all-reduce | flops 128 | bytes 1024 | tf_op jit(solution)/shard_map/pmax | solution.py:98
  352.2 0.9 fusion.58
  353.1 1.1 fusion.20
  354.2 34.0 %all-reduce = (f32[16,2,4,64]{3,2,1,0:T(4,128)S(1)}, f32[16,2,4]{2,1,0:T(2,128)S(1)}) all-reduce(f32[16,2,4,64]{3,2,1,0:T(4,128)S(1)} %fusion.20, f32[16,2,4]{2,1,0:T(2,128)S(1)} %fusion.58), channel_id=1, replica_groups=mesh['seq'=8,'tp'=4] {'seq'}, use_global_device_ids=true, to_apply=%region_20.21 | all-reduce | flops 8320 | bytes 66560 | tf_op jit(solution)/shard_map/psum | solution.py:107
  388.4 1.1 fusion.26
  389.5 5.2 all-gather.2
  394.8 30.5 %all_gather.44 = bf16[16,2048]{1,0:T(8,128)(2,1)S(1)} all-gather(bf16[16,256]{1,0:T(8,128)(2,1)S(1)} %add_convert_fusion.3), channel_id=1, replica_groups=mesh['seq'=8,'tp'=4] {'seq'}, dimensions={1}, use_global_device_ids=true | all-gather | bytes 73728 | tf_op jit(solution)/shard_map/all_gather | solution.py:67
  425.4 0.9 fusion.4
  426.4 2.3 fusion.6
  428.8 1.1 pad_maximum_fusion
  429.8 68.7 %all-reduce.9.cloned.1.call-done = (f32[16,2048]{1,0:T(8,128)}, f32[16,2048]{1,0:T(8,128)}) async-done(((f32[16,2048]{1,0:T(8,128)}, f32[16,2048]{1,0:T(8,128)}), (f32[16,2048]{1,0:T(8,128)}, f32[16,2048]{1,0:T(8,128)})) %all-reduce.9.cloned.1.call-update) | async-done | bytes 262160 | tf_op jit(solution)/shard_map/psum | solution.py:117
  498.5 1.2 fusion.2
  499.7 5.2 all-gather.3
  504.9 30.5 %all_gather.47 = bf16[16,2048]{1,0:T(8,128)(2,1)S(1)} all-gather(bf16[16,256]{1,0:T(8,128)(2,1)S(1)} %add_convert_fusion.2), channel_id=1, replica_groups=mesh['seq'=8,'tp'=4] {'seq'}, dimensions={1}, use_global_device_ids=true | all-gather | bytes 73728 | tf_op jit(solution)/shard_map/all_gather | solution.py:67
  535.4 0.6 copy.36
  (77 shorter events, 2.8 us)
Async XLA Ops:
  7.2 47.1 %slice-start = ((bf16[2,16,64,128]{3,2,1,0:T(8,128)(2,1)}), bf16[1,16,64,128]{3,2,1,0:T(8,128)(2,1)S(1)}, s32[]{:S(2)}) async-start(bf16[2,16,64,128]{3,2,1,0:T(8,128)(2,1)} %param.22), calls=%async_computation.2 | async-start | bytes 524288 | tf_op jit(solution)/shard_map/slice | solution.py:89
  7.2 48.1 %copy-start.15 = (s32[16]{0:T(128)S(1)}, s32[16]{0:T(128)}, u32[]{:S(2)}) copy-start(s32[16]{0:T(128)} %param.14) | copy-start | bytes 196
  7.2 48.5 %copy-start.13 = (s32[16]{0:T(128)S(1)}, s32[16]{0:T(128)}, u32[]{:S(2)}) copy-start(s32[16]{0:T(128)} %param.13) | copy-start | bytes 196
  7.2 228.5 %all-reduce.11.cloned.1.call-start = ((), (), s32[]{:S(2)}) async-start(), calls=%async_computation.1 | async-start | bytes 524288 | tf_op jit(solution)/shard_map/psum | solution.py:117
  53.6 0.7 copy-start.10
  54.3 71.6 %copy-start.7 = (bf16[2,512,256]{2,1,0:T(8,128)(2,1)S(1)}, bf16[2,512,256]{2,1,0:T(8,128)(2,1)}, u32[]{:S(2)}) copy-start(bf16[2,512,256]{2,1,0:T(8,128)(2,1)} %param.18) | copy-start | bytes 1572868
  55.5 107.1 %copy-start = (bf16[2,256,2048]{2,1,0:T(8,128)(2,1)S(1)}, bf16[2,256,2048]{2,1,0:T(8,128)(2,1)}, u32[]{:S(2)}) copy-start(bf16[2,256,2048]{2,1,0:T(8,128)(2,1)} %param.20) | copy-start | bytes 6291460
  55.7 107.8 %copy-start.9 = (pred[16,64]{1,0:T(8,128)(4,1)}, pred[16,64]{1,0:T(8,128)(4,1)S(1)}, u32[]{:S(2)}) copy-start(pred[16,64]{1,0:T(8,128)(4,1)S(1)} %get-tuple-element.34) | copy-start | bytes 3076
  55.7 107.8 %copy-start.12 = (pred[16,64]{1,0:T(8,128)(4,1)}, pred[16,64]{1,0:T(8,128)(4,1)S(1)}, u32[]{:S(2)}) copy-start(pred[16,64]{1,0:T(8,128)(4,1)S(1)} %get-tuple-element.35) | copy-start | bytes 3076
  163.6 151.0 %copy-start.1 = (bf16[2,16,64,128]{3,2,1,0:T(8,128)(2,1)S(1)}, bf16[2,16,64,128]{3,2,1,0:T(8,128)(2,1)}, u32[]{:S(2)}) copy-start(bf16[2,16,64,128]{3,2,1,0:T(8,128)(2,1)} %param.23) | copy-start | bytes 1572868
  163.6 151.0 %copy-start.2 = (bf16[2,16,64,128]{3,2,1,0:T(8,128)(2,1)S(1)}, bf16[2,16,64,128]{3,2,1,0:T(8,128)(2,1)}, u32[]{:S(2)}) copy-start(bf16[2,16,64,128]{3,2,1,0:T(8,128)(2,1)} %param.22) | copy-start | bytes 1572868
  165.9 332.6 %all-reduce.9.cloned.1.call-start = ((), (), s32[]{:S(2)}) async-start(), calls=%async_computation | async-start | bytes 524288 | tf_op jit(solution)/shard_map/psum | solution.py:117
  313.0 0.9 copy-start.11
  313.2 0.7 copy-start.8
  354.2 74.5 %copy-start.3 = (bf16[1,16,64,128]{3,2,1,0:T(8,128)(2,1)S(1)}, bf16[1,16,64,128]{3,2,1,0:T(8,128)(2,1)}, u32[]{:S(2)}) copy-start(bf16[1,16,64,128]{3,2,1,0:T(8,128)(2,1)} %get-tuple-element.17) | copy-start | bytes 786436
  354.2 74.5 %copy-start.4 = (bf16[1,16,64,128]{3,2,1,0:T(8,128)(2,1)S(1)}, bf16[1,16,64,128]{3,2,1,0:T(8,128)(2,1)}, u32[]{:S(2)}) copy-start(bf16[1,16,64,128]{3,2,1,0:T(8,128)(2,1)} %get-tuple-element.18) | copy-start | bytes 786436
  354.2 74.6 %copy-start.5 = (bf16[1,16,64,128]{3,2,1,0:T(8,128)(2,1)S(1)}, bf16[1,16,64,128]{3,2,1,0:T(8,128)(2,1)}, u32[]{:S(2)}) copy-start(bf16[1,16,64,128]{3,2,1,0:T(8,128)(2,1)} %get-tuple-element.32) | copy-start | bytes 786436
  354.2 74.6 %copy-start.6 = (bf16[1,16,64,128]{3,2,1,0:T(8,128)(2,1)S(1)}, bf16[1,16,64,128]{3,2,1,0:T(8,128)(2,1)}, u32[]{:S(2)}) copy-start(bf16[1,16,64,128]{3,2,1,0:T(8,128)(2,1)} %get-tuple-element.33) | copy-start | bytes 786436
  426.4 72.1 %copy-start.14 = (bf16[2,2048,256]{2,1,0:T(8,128)(2,1)S(1)}, bf16[2,2048,256]{2,1,0:T(8,128)(2,1)}, u32[]{:S(2)}) copy-start(bf16[2,2048,256]{2,1,0:T(8,128)(2,1)} %param.21) | copy-start | bytes 6291460
Sparse Core Ops, SparseCore 0:
  166.0 69.6 all-reduce.10
  428.8 69.5 all-reduce.8
